TPU v7x, 256 devices: a whole 4x4x8 slice. The times are simulated.
256 devices in a mesh: pb: 16 (over x_lo, z), ka: 16 (over x_hi, y, core).
Axes of the slice: x: 4 (x_hi: 2, x_lo: 2; x = x_hi * 2 + x_lo), y: 4, z: 8, core: 2. Of those that a mesh axis runs over, the one named last changes fastest.
Arguments:
- query_saved: bfloat16 [8192, 1024], P(('pb', 'ka')), may hold values from -6 to 6
- key_saved: bfloat16 [16384, 1024], P(('ka', 'pb')), may hold values from -6 to 6
- value_saved: bfloat16 [16384, 1024], P(('ka', 'pb')), may hold values from -6 to 6
- out_grad: bfloat16 [8192, 1024], P(('pb', 'ka')), may hold values from -768 to 768
- log_norm: bfloat16 [16, 8192], P(None, ('pb', 'ka')), as said below
- row_delta: bfloat16 [16, 8192], P(None, ('pb', 'ka')), may hold values from -1536 to 1536
- weight_query: bfloat16 [1024, 1024], replicated, may hold values from -0.1875 to 0.1875
- weight_key: bfloat16 [1024, 1024], replicated, may hold values from -0.1875 to 0.1875
- weight_value: bfloat16 [1024, 1024], replicated, may hold values from -0.1875 to 0.1875
Outputs:
- dx_query: bfloat16 [8192, 1024], P(('pb', 'ka'))
- dx_keyvalue: bfloat16 [16384, 1024], P(('ka', 'pb'))
Inputs may be any that keep to these rules, and one draw needn't show every extreme that they name: `log_norm`: each entry lies within 2 of 0.5 plus the natural logarithm of 16384.
All inputs are finite; a program needn't handle non-finite values.
Results may differ from a plain program's by a relative error of at most 0.008.
Values may be sent and summed in bfloat16 or wider, within the bound.
A program may use at most 128 MiB of HBM per device.

v0:
```python
import jax
import jax.numpy as jnp
from jax import lax
from jax.sharding import PartitionSpec as P

HEAD_DIM = 64


def turned_gather(arrays, axis, dims):
    turned = [jnp.moveaxis(a, dim, 0) for a, dim in zip(arrays, dims)]
    both = jnp.concatenate([t.reshape(len(t), -1) for t in turned], axis=1)
    whole, at, outs = (lax.all_gather(both, axis, axis=0, tiled=True), 0, [])
    for t, dim in zip(turned, dims):
        share = whole[:, at : at + t[0].size].reshape(-1, *t.shape[1:])
        outs.append(jnp.moveaxis(share, 0, dim))
        at += t[0].size
    return tuple(outs)


def in_one_piece(arrays, axis, dim, along):
    both = jnp.concatenate(arrays, axis=along)
    whole, at, outs = (lax.all_gather(both, axis, axis=dim, tiled=True), 0, [])
    for a in arrays:
        outs.append(lax.slice_in_dim(whole, at, at + a.shape[along], axis=along))
        at += a.shape[along]
    return tuple(outs)


def cut_along(array, dim, size):
    before, after = (array.shape[:dim], array.shape[dim + 1 :])
    return jnp.moveaxis(array.reshape(*before, size, -1, *after), dim, 0)


def summed_on_arrival(array, axis, dim):
    pieces = cut_along(array, dim, lax.axis_size(axis))
    arrived = lax.all_to_all(pieces, axis, split_axis=0, concat_axis=0, tiled=True)
    return arrived.sum(axis=0)


def project(grads, weights):
    contract = (((1,), (1,)), ((), ()))
    upper = grads.astype(jnp.bfloat16)
    lower = (grads - upper.astype(jnp.float32)).astype(jnp.bfloat16)
    first = lax.dot_general(upper, weights, contract, preferred_element_type=jnp.float32)
    return first + lax.dot_general(lower, weights, contract, preferred_element_type=jnp.float32)


def local(
    query_saved,
    key_saved,
    value_saved,
    out_grad,
    log_norm,
    row_delta,
    weight_query,
    weight_key,
    weight_value,
):
    query_block, grad_out_block, norm_block, delta_block = turned_gather(
        (query_saved, out_grad, log_norm, row_delta), "ka", (0, 0, 1, 1)
    )
    key_block, value_block = in_one_piece((key_saved, value_saved), "pb", 0, 1)
    query_rows = query_block.shape[0]
    key_rows = key_block.shape[0]
    model_width = query_block.shape[1]
    pair_width = 2 * HEAD_DIM
    pair_count = model_width // pair_width
    score_scale = 1.0 / HEAD_DIM**0.5

    def columns(source, row_count, column):
        return lax.dynamic_slice_in_dim(source, column, pair_width, 1).reshape(
            row_count, 2, HEAD_DIM
        )

    def head_pair(pair_index, totals):
        grad_query, grad_key, grad_value = totals
        column = pair_index * pair_width
        queries = columns(query_block, query_rows, column)
        grads_out = columns(grad_out_block, query_rows, column)
        keys_pair = columns(key_block, key_rows, column)
        values_pair = columns(value_block, key_rows, column)
        norm_pair = lax.dynamic_slice_in_dim(norm_block, pair_index * 2, 2, 0).astype(jnp.float32)
        delta_pair = lax.dynamic_slice_in_dim(delta_block, pair_index * 2, 2, 0).astype(jnp.float32)
        scores = (
            jnp.einsum("qhd,khd->hqk", queries, keys_pair, preferred_element_type=jnp.float32)
            * score_scale
        )
        probs = jnp.exp(scores - norm_pair[:, :, None])
        probs_b = probs.astype(jnp.bfloat16)
        grad_probs = jnp.einsum(
            "qhd,khd->hqk", grads_out, values_pair, preferred_element_type=jnp.float32
        )
        grad_scores = probs * (grad_probs - delta_pair[:, :, None])
        grad_scores_b = grad_scores.astype(jnp.bfloat16)
        value_part = jnp.einsum(
            "hqk,qhd->khd", probs_b, grads_out, preferred_element_type=jnp.float32
        )
        key_part = (
            jnp.einsum("hqk,qhd->khd", grad_scores_b, queries, preferred_element_type=jnp.float32)
            * score_scale
        )
        query_part = (
            jnp.einsum("hqk,khd->qhd", grad_scores_b, keys_pair, preferred_element_type=jnp.float32)
            * score_scale
        )
        grad_query = lax.dynamic_update_slice_in_dim(
            grad_query, query_part.reshape(query_rows, pair_width), column, 1
        )
        grad_key = lax.dynamic_update_slice_in_dim(
            grad_key, key_part.reshape(key_rows, pair_width), column, 1
        )
        grad_value = lax.dynamic_update_slice_in_dim(
            grad_value, value_part.reshape(key_rows, pair_width), column, 1
        )
        return (grad_query, grad_key, grad_value)

    start_totals = (
        jnp.zeros((query_rows, model_width), jnp.float32),
        jnp.zeros((key_rows, model_width), jnp.float32),
        jnp.zeros((key_rows, model_width), jnp.float32),
    )
    grad_query, grad_key, grad_value = lax.fori_loop(0, pair_count, head_pair, start_totals)
    query_owned = summed_on_arrival(grad_query, "ka", 0)
    dx_query = project(query_owned, weight_query).astype(jnp.bfloat16)
    combined = lax.psum_scatter(
        project(grad_key, weight_key) + project(grad_value, weight_value),
        "pb",
        scatter_dimension=0,
        tiled=True,
    )
    return (dx_query, combined.astype(jnp.bfloat16))


def solution(mesh):
    in_specs = (
        P(("pb", "ka"), None),
        P(("ka", "pb"), None),
        P(("ka", "pb"), None),
        P(("pb", "ka"), None),
        P(None, ("pb", "ka")),
        P(None, ("pb", "ka")),
        P(),
        P(),
        P(),
    )
    out_specs = (P(("pb", "ka"), None), P(("ka", "pb"), None))
    return jax.shard_map(local, mesh=mesh, in_specs=in_specs, out_specs=out_specs, check_vma=False)
```

profile of v0, /device:TPU:1, one launch (start us, length us, event | category | flops | bytes accessed | tf_op | source)
XLA Modules:
  0.0 404.5 jit_solution(9012038801444928533)
XLA Ops:
  12.4 55.4 %all-gather.5.cloned.1.call-done = bf16[512,2080]{1,0:T(8,128)(2,1)} async-done(((bf16[32,2080]{1,0:T(8,128)(2,1)}), bf16[512,2080]{1,0:T(8,128)(2,1)}) %all-gather.5.cloned.1.call-update) | async-done | bytes 2129936 | tf_op jit(solution)/shard_map/all_gather | solution.py:12
  69.0 3.1 fusion.20
  72.1 62.5 %all-gather.3.cloned.1.call-done = bf16[1024,2048]{1,0:T(8,128)(2,1)} async-done(((bf16[64,2048]{1,0:T(8,128)(2,1)}), bf16[1024,2048]{1,0:T(8,128)(2,1)}) %all-gather.3.cloned.1.call-update) | async-done | bytes 4194320 | tf_op jit(solution)/shard_map/all_gather | solution.py:22
  134.6 4.6 %fusion.19 = (bf16[1024,1024]{1,0:T(8,128)(2,1)}, bf16[1024,1024]{1,0:T(8,128)(2,1)}) fusion(bf16[1024,2048]{1,0:T(8,128)(2,1)} %all-gather.3.cloned.1.call-done), kind=kLoop, calls=%fused_computation.39 | loop fusion | bytes 8388608 | tf_op jit(solution)/shard_map/slice | solution.py:24
  145.7 145.1 %while.17 = (s32[]{:T(128)}, f32[512,1024]{1,0:T(8,128)}, f32[1024,1024]{0,1:T(8,128)}, f32[1024,1024]{0,1:T(8,128)}, bf16[1024,1024]{1,0:T(8,128)(2,1)}, /*inde...) while((s32[]{:T(128)}, f32[512,1024]{1,0:T(8,128)}, ...), condition=%wide.region_1.0_spmd, body=%wide.region_0.0_spmd.sunk | while | flops 679675904 | bytes 44589392 | solution.py:122
  152.8 3.4 multiply_convert_fusion.2
  159.2 3.1 fusion.64
  171.0 3.4 multiply_convert_fusion.2
  177.3 3.1 fusion.64
  189.1 3.4 multiply_convert_fusion.2
  195.4 3.1 fusion.64
  207.2 3.4 multiply_convert_fusion.2
  213.6 3.1 fusion.64
  225.3 3.4 multiply_convert_fusion.2
  231.7 3.1 fusion.64
  243.5 3.4 multiply_convert_fusion.2
  249.8 3.1 fusion.64
  261.6 3.4 multiply_convert_fusion.2
  267.9 3.1 fusion.64
  279.7 3.4 multiply_convert_fusion.2
  286.1 3.1 fusion.64
  290.8 4.7 %fusion.14 = f32[1024,1024]{1,0:T(8,128)S(1)} fusion(bf16[1024,1024]{1,0:T(8,128)(2,1)S(1)} %copy-done, f32[1024,1024]{0,1:T(8,128)} %get-tuple-element.174), kind=kOutput, calls=%fused_computation.30 | convolution fusion | flops 2148532224 | bytes 10485760 | tf_op jit(solution)/shard_map/dot_general | solution.py:44
  300.8 4.4 %add_add_fusion = f32[1024,1024]{1,0:T(8,128)} fusion(f32[1024,1024]{1,0:T(8,128)S(1)} %fusion.9, f32[1024,1024]{1,0:T(8,128)S(1)} %fusion.14, f32[1024,1024]{1,0:T(8,128)S(1)} %fusion.8, bf16[1024,1024]{1,0:T(8,128)(2,1)S(1)} %copy-done.5, f32[1024,1024]{0,1:T(8,128)S(1)} %copy-done.3), kind=kOutput, calls=%fused_computation.20 | convolution fusion | flops 2151677952 | bytes 23068672 | tf_op jit(solution)/shard_map/dot_general | solution.py:44
  305.2 84.1 %all_to_all.5 = f32[16,32,1024]{2,1,0:T(8,128)} all-to-all(f32[16,32,1024]{2,1,0:T(8,128)} %bitcast.77), channel_id=1, replica_groups=mesh['pb'=16,'ka'=16] {'ka'}, dimensions={0} | all-to-all | bytes 4194304 | tf_op jit(solution)/shard_map/all_to_all | solution.py:36
  (191 shorter events, 119.5 us)
Async XLA Ops:
  7.2 283.6 %copy-start = (bf16[1024,1024]{1,0:T(8,128)(2,1)S(1)}, bf16[1024,1024]{1,0:T(8,128)(2,1)}, u32[]{:S(2)}) copy-start(bf16[1024,1024]{1,0:T(8,128)(2,1)} %param.18) | copy-start | bytes 6291460
  7.2 60.6 %all-gather.5.cloned.1.call-start = ((), (), s32[]{:S(2)}) async-start(), calls=%async_computation.3 | async-start | bytes 2367488 | tf_op jit(solution)/shard_map/all_gather | solution.py:12
  10.5 124.0 %all-gather.3.cloned.1.call-start = ((), (), s32[]{:S(2)}) async-start(), calls=%async_computation.2 | async-start | bytes 4456448 | tf_op jit(solution)/shard_map/all_gather | solution.py:22
  12.3 384.0 %reduce-scatter.2.cloned.1.call-start = ((), (), s32[]{:S(2)}) async-start(), calls=%async_computation.4 | async-start | bytes 4456448 | tf_op jit(solution)/shard_map/reduce_scatter | solution.py:125
  156.2 1.3 copy-start.1
  158.4 3.9 copy-start.2
  174.3 1.3 copy-start.1
  176.5 3.9 copy-start.2
  192.4 1.3 copy-start.1
  194.7 3.8 copy-start.2
  210.6 1.3 copy-start.1
  212.8 3.9 copy-start.2
  228.7 1.3 copy-start.1
  230.9 3.8 copy-start.2
  246.8 1.3 copy-start.1
  249.0 3.8 copy-start.2
  264.9 1.3 copy-start.1
  267.2 3.9 copy-start.2
  283.1 1.3 copy-start.1
  285.3 3.9 copy-start.2
  290.8 4.7 %copy-start.4 = (f32[1024,1024]{0,1:T(8,128)S(1)}, f32[1024,1024]{0,1:T(8,128)}, u32[]{:S(2)}) copy-start(f32[1024,1024]{0,1:T(8,128)} %get-tuple-element.174) | copy-start | bytes 12582916
  295.5 2.4 copy-start.3
  295.5 2.9 copy-start.5
Sparse Core Ops, SparseCore 0:
  10.8 56.9 all-gather.4
  69.6 64.9 all-gather.2
  305.3 78.8 reduce-scatter.1
where the time goes:
time: 406 us; the launch traced here: 405 us
  waiting for transfers between devices  118 us (29%)
  matrix products  102 us (25%)
  blocking collectives  84.1 us (21%)
  local copies, waits for them, and re-layouts  79.9 us (20%)
  between operations  13.8 us (3%)
  other arithmetic  5.25 us (1%)
    all_to_all x1, blocking collectives, summed_on_arrival(): lax.all_to_all(pieces, axis, split_axis=0, concat_axis=0, tiled=True)  84.1 us
    all_gather x1, waiting for transfers between devices, in_one_piece(): whole, at, outs = (lax.all_gather(both, axis, axis=dim, tiled=True), 0, [])  62.5 us
    all_gather x1, waiting for transfers between devices, turned_gather(): whole, at, outs = (lax.all_gather(both, axis, axis=0, tiled=True), 0, [])  55.4 us
    dynamic_slice x64, local copies, waits for them, and re-layouts, columns(): lax.dynamic_slice_in_dim(source, column, pair_width, 1)  34.3 us
    dot_general x8, matrix products, head_pair(): jnp.einsum('qhd,khd->hqk', grads_out, values_pair, preferred_element_type...  26.8 us
    dot_general x8, matrix products, head_pair(): jnp.einsum('hqk,qhd->khd', probs_b, grads_out, preferred_element_type=jnp...  24.7 us
    dot_general x8, matrix products, head_pair(): jnp.einsum('qhd,khd->hqk', queries, keys_pair, preferred_element_type=jnp...  21.7 us
    dot_general x3, matrix products, project(): lax.dot_general(upper, weights, contract, preferred_element_type=jnp.floa...  11.4 us
  transfers between devices with their start and end apart: 3, of which 2 were waited for; matrix products, arithmetic and copies ran while one was open for 3% of the time, Pallas kernels for 0%

commit v1 on v0

--- a/solution.py
+++ b/solution.py
@@ -6,10 +6,15 @@
 HEAD_DIM = 64
 
 
+def swapped_in(value, mesh_axis, dim):
+    stack = jnp.stack([value] * lax.axis_size(mesh_axis))
+    return jnp.concatenate(lax.all_to_all(stack, mesh_axis, 0, 0), axis=dim)
+
+
 def turned_gather(arrays, axis, dims):
     turned = [jnp.moveaxis(a, dim, 0) for a, dim in zip(arrays, dims)]
     both = jnp.concatenate([t.reshape(len(t), -1) for t in turned], axis=1)
-    whole, at, outs = (lax.all_gather(both, axis, axis=0, tiled=True), 0, [])
+    whole, at, outs = (swapped_in(both, axis, 0), 0, [])
     for t, dim in zip(turned, dims):
         share = whole[:, at : at + t[0].size].reshape(-1, *t.shape[1:])
         outs.append(jnp.moveaxis(share, 0, dim))

time: 406 us -> 359 us (0.88)
  waiting for transfers between devices: 118 us -> 71.9 us
  blocking collectives: 84.1 us -> 69.8 us
  starting transfers between devices: 0.12 us -> 8.51 us
    all_to_all x0 -> x1, waiting for transfers between devices: none -> 71.9 us  [swapped_in(): return jnp.concatenate(lax.all_to_all(stack, mesh_axis, 0, 0), axis=dim)]
    all_gather x1, waiting for transfers between devices: 62.5 us -> 0.01 us  [in_one_piece(): whole, at, outs = (lax.all_gather(both, axis, axis=dim, tiled=True), 0, [])]
    all_gather x1 -> x0, waiting for transfers between devices: 55.4 us -> none  [turned_gather(): whole, at, outs = (lax.all_gather(both, axis, axis=0, tiled=True), 0, [])]
    all_to_all x1, blocking collectives: 84.1 us -> 69.8 us  [summed_on_arrival(): lax.all_to_all(pieces, axis, split_axis=0, concat_axis=0, tiled=True)]
    all_to_all x0 -> x1, starting transfers between devices: none -> 8.44 us  [swapped_in(): return jnp.concatenate(lax.all_to_all(stack, mesh_axis, 0, 0), axis=dim)]
  transfers between devices with their start and end apart: 3 -> 3, of which waited for: 2 -> 1; matrix products, arithmetic and copies ran while one was open for 3% -> 4% of each run, Pallas kernels for 0% -> 0%
where the time goes in v1:
time: 359 us; the launch traced here: 354 us
  matrix products  102 us (28%)
  local copies, waits for them, and re-layouts  80.6 us (22%)
  waiting for transfers between devices  71.9 us (20%)
  blocking collectives  69.8 us (19%)
  between operations  14.1 us (4%)
  starting transfers between devices  8.51 us (2%)
  other arithmetic  5.4 us (2%)
    all_to_all x1, waiting for transfers between devices, swapped_in(): return jnp.concatenate(lax.all_to_all(stack, mesh_axis, 0, 0), axis=dim)  71.9 us
    all_to_all x1, blocking collectives, summed_on_arrival(): lax.all_to_all(pieces, axis, split_axis=0, concat_axis=0, tiled=True)  69.8 us
    dynamic_slice x64, local copies, waits for them, and re-layouts, columns(): lax.dynamic_slice_in_dim(source, column, pair_width, 1)  34.3 us
    dot_general x8, matrix products, head_pair(): jnp.einsum('qhd,khd->hqk', grads_out, values_pair, preferred_element_type...  26.8 us
    dot_general x8, matrix products, head_pair(): jnp.einsum('hqk,qhd->khd', probs_b, grads_out, preferred_element_type=jnp...  24.7 us
    dot_general x8, matrix products, head_pair(): jnp.einsum('qhd,khd->hqk', queries, keys_pair, preferred_element_type=jnp...  21.7 us
    dot_general x3, matrix products, project(): lax.dot_general(upper, weights, contract, preferred_element_type=jnp.floa...  11.4 us
    while x32, local copies, waits for them, and re-layouts  10.5 us
  transfers between devices with their start and end apart: 3, of which 1 were waited for; matrix products, arithmetic and copies ran while one was open for 4% of the time, Pallas kernels for 0%

profile of v1, /device:TPU:1, one launch (start us, length us, event | category | flops | bytes accessed | tf_op | source)
XLA Modules:
  0.0 353.8 jit_solution(9259513250507385075)
XLA Ops:
  13.2 8.4 %all-to-all-start = ((bf16[16,32,2080]{2,1,0:T(8,128)(2,1)}), bf16[16,32,2080]{2,1,0:T(8,128)(2,1)}, u32[]{:S(2)}, u32[]{:S(2)}) async-start(bf16[16,32,2080]{2,1,0:T(8,128)(2,1)} %stack.2), calls=%async_computation | async-start | bytes 4456448 | tf_op jit(solution)/shard_map/all_to_all | solution.py:11
  21.7 71.9 %all-to-all-done = bf16[16,32,2080]{2,1,0:T(8,128)(2,1)} async-done(((bf16[16,32,2080]{2,1,0:T(8,128)(2,1)}), bf16[16,32,2080]{2,1,0:T(8,128)(2,1)}, u32[]{:S(2)}, u32[]{:S(2)}) %all-to-all-start) | async-done | bytes 2129952 | tf_op jit(solution)/shard_map/all_to_all | solution.py:11
  94.8 3.1 fusion.20
  97.9 4.6 %fusion.19 = (bf16[1024,1024]{1,0:T(8,128)(2,1)}, bf16[1024,1024]{1,0:T(8,128)(2,1)}) fusion(bf16[1024,2048]{1,0:T(8,128)(2,1)} %all-gather.2.cloned.1.call-done), kind=kLoop, calls=%fused_computation.39 | loop fusion | bytes 8388608 | tf_op jit(solution)/shard_map/slice | solution.py:29
  109.0 145.0 %while.17 = (s32[]{:T(128)}, f32[512,1024]{1,0:T(8,128)}, f32[1024,1024]{0,1:T(8,128)}, f32[1024,1024]{0,1:T(8,128)}, bf16[1024,1024]{1,0:T(8,128)(2,1)}, /*inde...) while((s32[]{:T(128)}, f32[512,1024]{1,0:T(8,128)}, ...), condition=%wide.region_1.0_spmd, body=%wide.region_0.0_spmd.sunk | while | flops 679675904 | bytes 44589392 | solution.py:127
  116.2 3.4 multiply_convert_fusion.2
  122.5 3.1 fusion.64
  134.3 3.4 multiply_convert_fusion.2
  140.6 3.1 fusion.64
  152.4 3.4 multiply_convert_fusion.2
  158.7 3.1 fusion.64
  170.5 3.4 multiply_convert_fusion.2
  176.8 3.1 fusion.64
  188.6 3.4 multiply_convert_fusion.2
  195.0 3.1 fusion.64
  206.7 3.4 multiply_convert_fusion.2
  213.1 3.1 fusion.64
  224.9 3.4 multiply_convert_fusion.2
  231.2 3.1 fusion.64
  243.0 3.4 multiply_convert_fusion.2
  249.3 3.1 fusion.64
  254.0 4.7 %fusion.14 = f32[1024,1024]{1,0:T(8,128)S(1)} fusion(bf16[1024,1024]{1,0:T(8,128)(2,1)S(1)} %copy-done, f32[1024,1024]{0,1:T(8,128)} %get-tuple-element.174), kind=kOutput, calls=%fused_computation.30 | convolution fusion | flops 2148532224 | bytes 10485760 | tf_op jit(solution)/shard_map/dot_general | solution.py:49
  264.0 4.4 %add_add_fusion = f32[1024,1024]{1,0:T(8,128)} fusion(f32[1024,1024]{1,0:T(8,128)S(1)} %fusion.9, f32[1024,1024]{1,0:T(8,128)S(1)} %fusion.14, f32[1024,1024]{1,0:T(8,128)S(1)} %fusion.8, bf16[1024,1024]{1,0:T(8,128)(2,1)S(1)} %copy-done.5, f32[1024,1024]{0,1:T(8,128)S(1)} %copy-done.3), kind=kOutput, calls=%fused_computation.20 | convolution fusion | flops 2151677952 | bytes 23068672 | tf_op jit(solution)/shard_map/dot_general | solution.py:49
  268.4 69.8 %all_to_all.10 = f32[16,32,1024]{2,1,0:T(8,128)} all-to-all(f32[16,32,1024]{2,1,0:T(8,128)} %bitcast.78), channel_id=1, replica_groups=mesh['pb'=16,'ka'=16] {'ka'}, dimensions={0} | all-to-all | bytes 4194304 | tf_op jit(solution)/shard_map/all_to_all | solution.py:41
  (191 shorter events, 120.3 us)
Async XLA Ops:
  7.2 246.8 %copy-start = (bf16[1024,1024]{1,0:T(8,128)(2,1)S(1)}, bf16[1024,1024]{1,0:T(8,128)(2,1)}, u32[]{:S(2)}) copy-start(bf16[1024,1024]{1,0:T(8,128)(2,1)} %param.18) | copy-start | bytes 6291460
  7.2 90.7 %all-gather.2.cloned.1.call-start = ((), (), s32[]{:S(2)}) async-start(), calls=%async_computation.3 | async-start | bytes 4456448 | tf_op jit(solution)/shard_map/all_gather | solution.py:27
  13.2 80.4 %all-to-all-start = ((bf16[16,32,2080]{2,1,0:T(8,128)(2,1)}), bf16[16,32,2080]{2,1,0:T(8,128)(2,1)}, u32[]{:S(2)}, u32[]{:S(2)}) async-start(bf16[16,32,2080]{2,1,0:T(8,128)(2,1)} %stack.2), calls=%async_computation | async-start | bytes 4456448 | tf_op jit(solution)/shard_map/all_to_all | solution.py:11
  21.6 323.7 %reduce-scatter.2.cloned.1.call-start = ((), (), s32[]{:S(2)}) async-start(), calls=%async_computation.4 | async-start | bytes 4456448 | tf_op jit(solution)/shard_map/reduce_scatter | solution.py:130
  119.5 1.3 copy-start.1
  121.7 3.9 %copy-start.2 = (bf16[2,512,1024]{2,1,0:T(8,128)(2,1)S(1)}, bf16[2,512,1024]{2,1,0:T(8,128)(2,1)}, u32[]{:S(2)}) copy-start(bf16[2,512,1024]{2,1,0:T(8,128)(2,1)} %copy-done.1) | copy-start | bytes 6291460 | tf_op jit(solution)/shard_map/while
  137.6 1.3 copy-start.1
  139.8 3.9 %copy-start.2 = (bf16[2,512,1024]{2,1,0:T(8,128)(2,1)S(1)}, bf16[2,512,1024]{2,1,0:T(8,128)(2,1)}, u32[]{:S(2)}) copy-start(bf16[2,512,1024]{2,1,0:T(8,128)(2,1)} %copy-done.1) | copy-start | bytes 6291460 | tf_op jit(solution)/shard_map/while
  155.7 1.3 copy-start.1
  157.9 3.9 %copy-start.2 = (bf16[2,512,1024]{2,1,0:T(8,128)(2,1)S(1)}, bf16[2,512,1024]{2,1,0:T(8,128)(2,1)}, u32[]{:S(2)}) copy-start(bf16[2,512,1024]{2,1,0:T(8,128)(2,1)} %copy-done.1) | copy-start | bytes 6291460 | tf_op jit(solution)/shard_map/while
  173.9 1.3 copy-start.1
  176.1 3.9 %copy-start.2 = (bf16[2,512,1024]{2,1,0:T(8,128)(2,1)S(1)}, bf16[2,512,1024]{2,1,0:T(8,128)(2,1)}, u32[]{:S(2)}) copy-start(bf16[2,512,1024]{2,1,0:T(8,128)(2,1)} %copy-done.1) | copy-start | bytes 6291460 | tf_op jit(solution)/shard_map/while
  192.0 1.3 copy-start.1
  194.2 3.9 %copy-start.2 = (bf16[2,512,1024]{2,1,0:T(8,128)(2,1)S(1)}, bf16[2,512,1024]{2,1,0:T(8,128)(2,1)}, u32[]{:S(2)}) copy-start(bf16[2,512,1024]{2,1,0:T(8,128)(2,1)} %copy-done.1) | copy-start | bytes 6291460 | tf_op jit(solution)/shard_map/while
  210.1 1.3 copy-start.1
  212.3 3.9 %copy-start.2 = (bf16[2,512,1024]{2,1,0:T(8,128)(2,1)S(1)}, bf16[2,512,1024]{2,1,0:T(8,128)(2,1)}, u32[]{:S(2)}) copy-start(bf16[2,512,1024]{2,1,0:T(8,128)(2,1)} %copy-done.1) | copy-start | bytes 6291460 | tf_op jit(solution)/shard_map/while
  228.2 1.3 copy-start.1
  230.4 3.8 %copy-start.2 = (bf16[2,512,1024]{2,1,0:T(8,128)(2,1)S(1)}, bf16[2,512,1024]{2,1,0:T(8,128)(2,1)}, u32[]{:S(2)}) copy-start(bf16[2,512,1024]{2,1,0:T(8,128)(2,1)} %copy-done.1) | copy-start | bytes 6291460 | tf_op jit(solution)/shard_map/while
  246.3 1.3 copy-start.1
  248.5 3.9 %copy-start.2 = (bf16[2,512,1024]{2,1,0:T(8,128)(2,1)S(1)}, bf16[2,512,1024]{2,1,0:T(8,128)(2,1)}, u32[]{:S(2)}) copy-start(bf16[2,512,1024]{2,1,0:T(8,128)(2,1)} %copy-done.1) | copy-start | bytes 6291460 | tf_op jit(solution)/shard_map/while
  254.0 4.7 %copy-start.4 = (f32[1024,1024]{0,1:T(8,128)S(1)}, f32[1024,1024]{0,1:T(8,128)}, u32[]{:S(2)}) copy-start(f32[1024,1024]{0,1:T(8,128)} %get-tuple-element.174) | copy-start | bytes 12582916
  258.7 2.4 copy-start.3
  258.8 2.9 copy-start.5
Sparse Core Ops, SparseCore 0:
  9.8 71.3 all-gather.1
  268.6 70.8 reduce-scatter.1
